TPU v7x, 512 devices: a whole 4x4x16 slice. The times are simulated.
512 devices in a mesh: cfg: 2 (over x_lo), seq: 256 (over y, x_hi, z, core).
Axes of the slice: x: 4 (x_hi: 2, x_lo: 2; x = x_hi * 2 + x_lo), y: 4, z: 16, core: 2. Of those that a mesh axis runs over, the one named last changes fastest.
Arguments:
- img_queries: bfloat16 [2, 3072, 1216], P('cfg', 'seq')
- img_keys: bfloat16 [2, 3072, 1216], P('cfg', 'seq')
- img_values: bfloat16 [2, 3072, 1216], P('cfg', 'seq'), may hold values from -6 to 6
- text_keys: bfloat16 [2, 256, 1216], P('cfg', 'seq'), may hold values from -6 to 6
- text_values: bfloat16 [2, 256, 1216], P('cfg', 'seq'), may hold values from -18 to 18
- query_gain: float32 [64], replicated, may hold values from 0.5 to 8, as said below
- key_gain: float32 [64], replicated, may hold values from 0.5 to 8, as said below
- text_gain: float32 [64], replicated, may hold values from 0.5 to 8, as said below
- text_lengths: int32 [2], P('cfg'), may hold values from 1 to 256, as said below
- text_blocks: int32 [2, 256], P('cfg', 'seq'), may hold values from 0 to 1
- latent: float32 [3072, 64], P('seq', 'cfg'), may hold values from -6 to 6
- base_velocity: bfloat16 [2, 3072, 64], P('cfg', 'seq'), may hold values from -6 to 6
- out_weight: bfloat16 [1216, 64], replicated, may hold values from -1.25 to 1.25
- timestep: int32 [1], replicated, may hold values from 0 to 27
Outputs:
- next_latent: float32 [3072, 64], P('seq', 'cfg')
- denoised: float32 [3072, 64], P('seq', 'cfg')
Inputs may be any that keep to these rules, and one draw needn't show every extreme that they name: `query_gain`: gains are positive. `key_gain`: gains are positive. `text_gain`: gains are positive. `text_lengths`: one of the two halves has all 256 slots within its length.
All inputs are finite; a program needn't handle non-finite values.
Results may differ from a plain program's by a relative error of at most 0.007.
The roundings to bfloat16 on the way count: a program that leaves them out, or rounds other values in their place, can miss the bound.
Values may be sent and summed in bfloat16 or wider, within the bound.
No kernel may reach another device: no remote copies, remote signals or barrier semaphores. Data moves between devices by JAX's collectives and lax.ppermute only.
A program may use at most 128 MiB of HBM per device.

v0:
```python
import math
import jax
import jax.numpy as jnp
from jax import lax
from jax.sharding import PartitionSpec as P

STEPS = 28
epsilon = 1e-06
guidance = 3.5
shift_factor = 3.0
masked_score = -1e30


def from_partner(block, axis, stride):
    count = lax.axis_size(axis)
    route = []
    for low in range(count):
        high = low | 1 << stride
        if high != low and high < count:
            route += [(low, high), (high, low)]
    return lax.ppermute(block, axis, route)


def head_norm(values, gain_row):
    widened = values.astype(jnp.float32).reshape(values.shape[0], -1, gain_row.shape[0])
    scaled = (
        widened
        * lax.rsqrt(jnp.mean(widened * widened, axis=-1, keepdims=True) + epsilon)
        * gain_row
    )
    return scaled.astype(jnp.bfloat16)


def sigma_at(position):
    time_left = 1.0 - position / STEPS
    return shift_factor * time_left / (1.0 + (shift_factor - 1.0) * time_left)


def attend_block(running, queries, keys_block, values_block, usable):
    run_max, run_total, run_sum = running
    head_count = queries.shape[1]
    head_size = queries.shape[2]
    keys_heads = keys_block.reshape(keys_block.shape[0], head_count, head_size)
    values_heads = values_block.reshape(values_block.shape[0], head_count, head_size)
    scores = jnp.einsum("rhd,khd->hrk", queries, keys_heads, preferred_element_type=jnp.float32) * (
        1.0 / math.sqrt(head_size)
    )
    scores = jnp.where(usable[None, None, :], scores, masked_score)
    new_max = jnp.maximum(run_max, jnp.max(scores, axis=-1))
    factor = jnp.exp(run_max - new_max)
    weights_block = jnp.where(usable[None, None, :], jnp.exp(scores - new_max[..., None]), 0.0)
    run_total = run_total * factor + jnp.sum(weights_block, axis=-1)
    run_sum = run_sum * factor[..., None] + jnp.einsum(
        "hrk,khd->hrd",
        weights_block.astype(jnp.bfloat16),
        values_heads,
        preferred_element_type=jnp.float32,
    )
    return (new_max, run_total, run_sum)


def attend_text(running, queries, keys_block, values_block, usable_flags):
    usable = usable_flags == 1

    def take_block(state_in):
        return attend_block(state_in, queries, keys_block, values_block, usable)

    def keep_state(state_in):
        return state_in

    return lax.cond(jnp.any(usable), take_block, keep_state, running)


def on_device(
    img_queries,
    img_keys,
    img_values,
    text_keys,
    text_values,
    query_gain,
    key_gain,
    text_gain,
    text_lengths,
    text_blocks,
    latent,
    base_velocity,
    out_weight,
    timestep,
):
    head_size = query_gain.shape[0]
    head_count = img_queries.shape[2] // head_size
    row_count = img_queries.shape[1]
    text_count = text_keys.shape[1]
    queries = head_norm(img_queries[0], query_gain)
    keys_local = head_norm(img_keys[0], key_gain).reshape(row_count, head_count * head_size)
    values_local = img_values[0]
    text_keys_local = head_norm(text_keys[0], text_gain).reshape(text_count, head_count * head_size)
    text_values_local = text_values[0]
    slot_index = lax.axis_index("seq") * text_count + jnp.arange(text_count, dtype=jnp.int32)
    usable_text = ((slot_index < text_lengths[0]) & (text_blocks[0, 0] == 1)).astype(jnp.int32)
    initial = (
        jnp.full((head_count, row_count), masked_score, jnp.float32),
        jnp.zeros((head_count, row_count), jnp.float32),
        jnp.zeros((head_count, row_count, head_size), jnp.float32),
    )
    running = initial
    key_piece = lax.all_gather(keys_local, "seq", axis=0, tiled=True)
    value_piece = lax.all_gather(values_local, "seq", axis=0, tiled=True)
    text_key_piece = lax.all_gather(text_keys_local, "seq", axis=0, tiled=True)
    text_value_piece = lax.all_gather(text_values_local, "seq", axis=0, tiled=True)
    usable_piece = lax.all_gather(usable_text, "seq", axis=0, tiled=True)
    every_key = jnp.ones((key_piece.shape[0],), dtype=jnp.bool_)
    running = attend_block(running, queries, key_piece, value_piece, every_key)
    final_state = attend_text(running, queries, text_key_piece, text_value_piece, usable_piece)
    run_max, run_total, run_sum = final_state
    attended = (
        (run_sum / run_total[..., None])
        .transpose(1, 0, 2)
        .reshape(row_count, head_count * head_size)
        .astype(jnp.bfloat16)
    )
    velocity = base_velocity[0].astype(jnp.float32) + jnp.dot(
        attended, out_weight, preferred_element_type=jnp.float32
    )
    guide_half = lax.axis_index("cfg")
    half_width = latent.shape[1]
    own_part = lax.dynamic_slice_in_dim(velocity, guide_half * half_width, half_width, 1)
    sent_part = lax.dynamic_slice_in_dim(velocity, (1 - guide_half) * half_width, half_width, 1)
    partner = from_partner(sent_part, "cfg", 0)
    cond_part = jnp.where(guide_half == 0, own_part, partner)
    uncond_part = jnp.where(guide_half == 0, partner, own_part)
    guided = uncond_part + guidance * (cond_part - uncond_part)
    step_now = timestep[0].astype(jnp.float32)
    sigma_now = sigma_at(step_now)
    sigma_next = sigma_at(step_now + 1.0)
    next_latent = latent + (sigma_next - sigma_now) * guided
    denoised = latent - sigma_now * guided
    return (next_latent, denoised)


def solution(mesh):
    return jax.shard_map(
        on_device,
        mesh=mesh,
        in_specs=(
            P("cfg", "seq", None),
            P("cfg", "seq", None),
            P("cfg", "seq", None),
            P("cfg", "seq", None),
            P("cfg", "seq", None),
            P(),
            P(),
            P(),
            P("cfg"),
            P("cfg", "seq"),
            P("seq", "cfg"),
            P("cfg", "seq", None),
            P(),
            P(),
        ),
        out_specs=(P("seq", "cfg"), P("seq", "cfg")),
        check_vma=False,
    )
```

profile of v0, /device:TPU:1, one launch (start us, length us, event | category | flops | bytes accessed | tf_op | source)
XLA Modules:
  0.0 1482.1 jit_solution(14273524936408419100)
XLA Ops:
  7.2 0.8 convert_multiply_fusion
  8.5 0.7 mul.197
  9.2 1.4 fusion.27
  10.7 1.4 copy.44
  13.4 1.3 dynamic-slice
  14.7 0.7 fusion.33
  15.5 655.9 %all-reduce = s32[256]{0:T(256)S(1)} all-reduce(s32[256]{0:T(256)S(1)} %fusion.33), channel_id=1, replica_groups=mesh['cfg'=2,'seq'=256] {'seq'}, use_global_device_ids=true, to_apply=%add | all-reduce | flops 256 | bytes 2048
  671.3 0.6 fusion.35
  672.6 0.9 reshape.183
  673.5 0.7 mul.209
  674.2 0.7 fusion.31
  675.0 0.1 reduce_sum.48
  675.3 0.7 fusion.30
  676.0 358.8 %all-gather.3 = bf16[256,1,1216]{2,1,0:T(2,128)(2,1)S(1)} all-gather(bf16[1,1,1216]{2,1,0:T(2,128)(2,1)S(1)} %fusion.30), channel_id=1, replica_groups=mesh['cfg'=2,'seq'=256] {'seq'}, dimensions={0}, use_global_device_ids=true | all-gather | bytes 625024 | tf_op jit(solution)/shard_map/all_gather | solution.py:109
  1034.8 1.3 copy.46
  1036.1 353.9 %all-gather.1 = bf16[256,1,1216]{2,1,0:T(2,128)(2,1)S(1)} all-gather(bf16[1,1,1216]{2,1,0:T(2,128)(2,1)S(1)} %copy-done.2), channel_id=3, replica_groups=mesh['cfg'=2,'seq'=256] {'seq'}, dimensions={0}, use_global_device_ids=true | all-gather | bytes 625024 | tf_op jit(solution)/shard_map/all_gather | solution.py:110
  1389.9 1.3 copy.47
  1391.5 24.8 %reshape.174 = bf16[3072,19,64]{2,1,0:T(8,128)(2,1)} reshape(bf16[256,12,1216]{2,1,0:T(8,128)(2,1)} %all-gather.9.cloned.1.call-done) | data formatting | bytes 14942208 | tf_op jit(solution)/shard_map/reshape | solution.py:43
  1416.3 12.3 fusion.37
  1428.5 2.7 fusion.15
  1431.3 31.0 %copy.45 = bf16[1,3072,1216]{1,2,0:T(8,128)(2,1)} copy(bf16[1,3072,1216]{2,0,1:T(2,128)(2,1)} %all-gather.7.cloned.1.call-done) | data formatting | bytes 14942208 | tf_op jit(solution)/shard_map/all_gather | solution.py:108
  1462.3 6.4 fusion.19
  1468.7 0.9 conditional.1
  1468.8 0.3 fusion.36
  1469.1 0.2 fusion.2
  1469.3 0.3 convolution_add_fusion
  1469.6 0.1 fusion.26
  1469.8 0.1 convert_element_type.127
  1469.9 0.2 convolution_add_fusion.1
  1470.2 2.2 collective-permute-start
  1473.2 1.4 collective-permute-done
  1474.6 0.7 multiply_subtract_fusion
  (37 shorter events, 1.3 us)
Async XLA Ops:
  7.2 1462.7 %copy-start = (bf16[1216,64]{0,1:T(8,128)(2,1)S(1)}, bf16[1216,64]{0,1:T(8,128)(2,1)}, u32[]{:S(2)}) copy-start(bf16[1216,64]{0,1:T(8,128)(2,1)} %param.28) | copy-start | bytes 466948
  7.2 1028.9 %copy-start.2 = (bf16[1,1,1216]{2,1,0:T(2,128)(2,1)S(1)}, bf16[1,1,1216]{2,1,0:T(2,128)(2,1)}, u32[]{:S(2)}) copy-start(bf16[1,1,1216]{2,1,0:T(2,128)(2,1)} %param.20) | copy-start | bytes 7300
  7.2 1384.3 %all-gather.9.cloned.1.call-start = ((), (), s32[]{:S(2)}) async-start(), calls=%async_computation.1 | async-start | bytes 10526720 | tf_op jit(solution)/shard_map/all_gather | solution.py:107
  8.4 1382.9 %copy-start.4 = (f32[64]{0:T(128)S(1)}, f32[64]{0:T(128)}, u32[]{:S(2)}) copy-start(f32[64]{0:T(128)} %param.21) | copy-start | bytes 772
  10.6 1420.7 %all-gather.7.cloned.1.call-start = ((), (), s32[]{:S(2)}) async-start(), calls=%async_computation | async-start | bytes 15790080 | tf_op jit(solution)/shard_map/all_gather | solution.py:108
  1462.3 7.6 copy-start.3
  1462.3 12.2 copy-start.1
  1470.2 4.4 collective-permute-start
Sparse Core Ops, SparseCore 0:
  12.5 234.6 all-gather.8
  252.0 238.5 all-gather.6
where the time goes:
time: 1480 us
  blocking collectives  1370 us (93%)
  local copies, waits for them, and re-layouts  64.1 us (4%)
  matrix products  19.4 us (1%)
  between operations  16.9 us (1%)
    unnamed x1, blocking collectives  656 us
    all_gather x1, blocking collectives, on_device(): text_key_piece = lax.all_gather(text_keys_local, 'seq', axis=0, tiled=True)  359 us
    all_gather x1, blocking collectives, on_device(): lax.all_gather(text_values_local, 'seq', axis=0, tiled=True)  354 us
    all_gather x1, local copies, waits for them, and re-layouts, on_device(): value_piece = lax.all_gather(values_local, 'seq', axis=0, tiled=True)  31 us
  transfers between devices with their start and end apart: 3, of which 1 were waited for; matrix products, arithmetic and copies ran while one was open for 3% of the time, Pallas kernels for 0%

commit v1 on v0

--- a/solution.py
+++ b/solution.py
@@ -107,7 +107,9 @@
     key_piece = lax.all_gather(keys_local, "seq", axis=0, tiled=True)
     value_piece = lax.all_gather(values_local, "seq", axis=0, tiled=True)
     text_key_piece = lax.all_gather(text_keys_local, "seq", axis=0, tiled=True)
-    text_value_piece = lax.all_gather(text_values_local, "seq", axis=0, tiled=True)
+    text_value_piece = jnp.concatenate(
+        lax.all_to_all(jnp.stack([text_values_local] * lax.axis_size("seq")), "seq", 0, 0), axis=0
+    )
     usable_piece = lax.all_gather(usable_text, "seq", axis=0, tiled=True)
     every_key = jnp.ones((key_piece.shape[0],), dtype=jnp.bool_)
     running = attend_block(running, queries, key_piece, value_piece, every_key)

time: 1480 us -> 1170 us (0.79)
  blocking collectives: 1370 us -> 1020 us
  starting transfers between devices: 2.33 us -> 27.2 us
    all_gather x1 -> x0, blocking collectives: 354 us -> none  [on_device(): lax.all_gather(text_values_local, 'seq', axis=0, tiled=True)]
    all_to_all x0 -> x1, starting transfers between devices: none -> 24.5 us  [on_device(): lax.all_to_all(jnp.stack([text_values_local] * lax.axis_size('seq')), 'se...]
  transfers between devices with their start and end apart: 3 -> 4, of which waited for: 1 -> 1; matrix products, arithmetic and copies ran while one was open for 3% -> 5% of each run, Pallas kernels for 0% -> 0%
where the time goes in v1:
time: 1170 us
  blocking collectives  1020 us (87%)
  local copies, waits for them, and re-layouts  66.5 us (6%)
  starting transfers between devices  27.2 us (2%)
  matrix products  19.4 us (2%)
  between operations  17 us (1%)
  other arithmetic  13.4 us (1%)
    unnamed x1, blocking collectives  668 us
    all_gather x1, blocking collectives, on_device(): text_key_piece = lax.all_gather(text_keys_local, 'seq', axis=0, tiled=True)  353 us
    all_gather x1, local copies, waits for them, and re-layouts, on_device(): value_piece = lax.all_gather(values_local, 'seq', axis=0, tiled=True)  31 us
    reshape x1, local copies, waits for them, and re-layouts, attend_block(): keys_heads = keys_block.reshape(keys_block.shape[0], head_count, head_size)  24.8 us
    all_to_all x1, starting transfers between devices, on_device(): lax.all_to_all(jnp.stack([text_values_local] * lax.axis_size('seq')), 'se...  24.5 us
  transfers between devices with their start and end apart: 4, of which 1 were waited for; matrix products, arithmetic and copies ran while one was open for 5% of the time, Pallas kernels for 0%

profile of v1, /device:TPU:1, one launch (start us, length us, event | category | flops | bytes accessed | tf_op | source)
XLA Modules:
  0.0 1165.1 jit_solution(10318169095163260236)
XLA Ops:
  7.3 0.8 convert_multiply_fusion
  8.5 0.7 mul.197
  9.2 1.4 fusion.27
  10.7 1.4 copy.41
  12.2 0.7 reduce.3
  12.9 0.7 stack.3
  13.6 0.5 broadcast.103
  14.1 4.8 reduce.5
  18.9 1.5 reshape.204
  20.4 24.5 %all-to-all-start = ((bf16[256,2,608]{2,1,0:T(2,128)(2,1)}), bf16[256,2,608]{2,1,0:T(2,128)(2,1)S(1)}, u32[]{:S(2)}, u32[]{:S(2)}) async-start(bf16[256,2,608]{2,1,0:T(2,128)(2,1)} %reshape.204), calls=%async_computation | async-start | bytes 1310720 | tf_op jit(solution)/shard_map/all_to_all | solution.py:111
  46.3 1.3 dynamic-slice
  47.5 0.7 fusion.33
  48.3 667.6 %all-reduce = s32[256]{0:T(256)S(1)} all-reduce(s32[256]{0:T(256)S(1)} %fusion.33), channel_id=1, replica_groups=mesh['cfg'=2,'seq'=256] {'seq'}, use_global_device_ids=true, to_apply=%add | all-reduce | flops 256 | bytes 2048
  715.9 0.6 fusion.35
  717.8 352.8 %all-gather.2 = bf16[256,1,1216]{2,1,0:T(2,128)(2,1)S(1)} all-gather(bf16[1,1,1216]{2,1,0:T(2,128)(2,1)S(1)} %fusion.30), channel_id=1, replica_groups=mesh['cfg'=2,'seq'=256] {'seq'}, dimensions={0}, use_global_device_ids=true | all-gather | bytes 625024 | tf_op jit(solution)/shard_map/all_gather | solution.py:109
  1070.6 1.3 copy.43
  1072.1 1.1 reshape.205
  1073.2 24.8 %reshape.174 = bf16[3072,19,64]{2,1,0:T(8,128)(2,1)} reshape(bf16[256,12,1216]{2,1,0:T(8,128)(2,1)} %all-gather.8.cloned.1.call-done) | data formatting | bytes 14942208 | tf_op jit(solution)/shard_map/reshape | solution.py:43
  1098.0 12.3 %fusion.37 = (f32[19,12]{1,0:T(8,128)S(1)}, f32[19,12,3072]{2,1,0:T(8,128)}) fusion(bf16[3072,19,64]{2,1,0:T(8,128)(2,1)} %reshape.174, bf16[12,19,64]{2,1,0:T(8,128)(2,1)S(1)} %multiply_convert_fusion), kind=kOutput, calls=%fused_computation.56 | convolution fusion | flops 91053856 | bytes 10302864 | tf_op jit(solution)/shard_map/rhd,khd->hrk/dot_general | solution.py:45
  1110.2 2.7 fusion.15
  1113.0 31.0 %copy.42 = bf16[1,3072,1216]{1,2,0:T(8,128)(2,1)} copy(bf16[1,3072,1216]{2,0,1:T(2,128)(2,1)} %all-gather.6.cloned.1.call-done) | data formatting | bytes 14942208 | tf_op jit(solution)/shard_map/all_gather | solution.py:108
  1144.1 6.4 fusion.19
  1150.5 2.2 conditional.1
  1150.5 0.3 fusion.36
  1150.8 0.2 fusion.2
  1151.0 1.3 copy.45
  1152.3 0.3 convolution_add_fusion
  1152.6 0.1 fusion.26
  1152.9 0.2 convolution_add_fusion.1
  1153.2 2.6 collective-permute-start
  1156.5 1.1 collective-permute-done
  1157.6 0.7 multiply_subtract_fusion
  (48 shorter events, 1.7 us)
Async XLA Ops:
  7.2 1145.8 %copy-start = (bf16[1216,64]{0,1:T(8,128)(2,1)S(1)}, bf16[1216,64]{0,1:T(8,128)(2,1)}, u32[]{:S(2)}) copy-start(bf16[1216,64]{0,1:T(8,128)(2,1)} %param.28) | copy-start | bytes 466948
  7.2 710.0 %copy-start.1 = (bf16[1,12,1216]{2,1,0:T(8,128)(2,1)S(1)}, bf16[1,12,1216]{2,1,0:T(8,128)(2,1)}, u32[]{:S(2)}) copy-start(bf16[1,12,1216]{2,1,0:T(8,128)(2,1)} %param.16) | copy-start | bytes 87556
  7.2 710.1 %copy-start.6 = (f32[64]{0:T(128)S(1)}, f32[64]{0:T(128)}, u32[]{:S(2)}) copy-start(f32[64]{0:T(128)} %param.23) | copy-start | bytes 772
  7.2 710.2 %copy-start.2 = (bf16[1,1,1216]{2,1,0:T(2,128)(2,1)S(1)}, bf16[1,1,1216]{2,1,0:T(2,128)(2,1)}, u32[]{:S(2)}) copy-start(bf16[1,1,1216]{2,1,0:T(2,128)(2,1)} %param.19) | copy-start | bytes 7300
  7.2 1066.0 %all-gather.8.cloned.1.call-start = ((), (), s32[]{:S(2)}) async-start(), calls=%async_computation.2 | async-start | bytes 10526720 | tf_op jit(solution)/shard_map/all_gather | solution.py:107
  10.7 1102.4 %all-gather.6.cloned.1.call-start = ((), (), s32[]{:S(2)}) async-start(), calls=%async_computation.1 | async-start | bytes 15790080 | tf_op jit(solution)/shard_map/all_gather | solution.py:108
  14.1 1057.9 %copy-start.5 = (f32[64]{0:T(128)S(1)}, f32[64]{0:T(128)}, u32[]{:S(2)}) copy-start(f32[64]{0:T(128)} %param.21) | copy-start | bytes 772
  20.4 1051.7 %all-to-all-start = ((bf16[256,2,608]{2,1,0:T(2,128)(2,1)}), bf16[256,2,608]{2,1,0:T(2,128)(2,1)S(1)}, u32[]{:S(2)}, u32[]{:S(2)}) async-start(bf16[256,2,608]{2,1,0:T(2,128)(2,1)} %reshape.204), calls=%async_computation | async-start | bytes 1310720 | tf_op jit(solution)/shard_map/all_to_all | solution.py:111
  1150.4 2.5 copy-start.4
  1150.4 7.1 copy-start.3
  1153.2 4.4 collective-permute-start
Sparse Core Ops, SparseCore 0:
  12.5 235.9 all-gather.7
  253.2 238.8 all-gather.5
